TPU v7x, 256 devices: a whole 4x4x8 slice. The times are simulated.
256 devices in a mesh: seq: 32 (over x, z), tp: 8 (over y, core).
Axes of the slice: x: 4, y: 4, z: 8, core: 2. Of those that a mesh axis runs over, the one named last changes fastest.
Arguments:
- tokens: bfloat16 [16384, 5376], P('seq'), may hold values from -6 to 6
- query_weight: bfloat16 [5376, 2048], P(None, 'tp')
- key_weight: bfloat16 [5376, 1024], P(None, 'tp')
- value_weight: bfloat16 [5376, 1024], P(None, 'tp'), may hold values from -0.078125 to 0.078125
- query_norm_gain: float32 [128], replicated, as said below
- key_norm_gain: float32 [128], replicated, as said below
- adapter_down_weight: bfloat16 [32, 5376, 64], P('seq', 'tp'), may hold values from -0.078125 to 0.078125
- adapter_up_weight: bfloat16 [32, 64, 2048], P('seq', None, 'tp'), may hold values from -0.75 to 0.75
- token_adapter_index: int32 [16384, 1], P('seq'), may hold values from 0 to 31; in each aligned block of 512 rows (0 to 511, 512 to 1023, ...) at most 32 rows name the same one
- packed_prompt_length: int32 [16], replicated, may hold values from 1 to 2048, 16384 in all
Outputs:
- attended: bfloat16 [16384, 2048], P('seq', 'tp')
Inputs may be any that keep to these rules, and one draw needn't show every extreme that they name: `token_adapter_index`: in each aligned block of 512 rows (the rows of one index of seq) no adapter is named by more than 32 rows, a bound that some block reaches. `packed_prompt_length`: they sum to 16384; the largest is exactly 2048. `query_norm_gain`: positive gains. `key_norm_gain`: positive gains.
All inputs are finite; a program needn't handle non-finite values.
Results may differ from a plain program's by a relative error of at most 0.02.
Values may be sent and summed in bfloat16 or wider, within the bound.
No kernel may reach another device: no remote copies, remote signals or barrier semaphores. Data moves between devices by JAX's collectives and lax.ppermute only.
A program may use at most 64 MiB of HBM per device.

v0:
```python
import jax
import jax.numpy as jnp
from jax import lax
from jax.sharding import PartitionSpec as P

WINDOW = 1024
query_scale = 0.07715167498104596


def passed_along(block, axis, distance):
    devices = range(lax.axis_size(axis))
    route = [(i - distance, i) for i in devices if i - distance in devices]
    return lax.ppermute(block, axis, route)


def make_dispatch(adapter_of, adapter_total, capacity):
    one_hot = (adapter_of[:, None] == jnp.arange(adapter_total, dtype=jnp.int32)[None, :]).astype(
        jnp.int32
    )
    before = jnp.cumsum(one_hot, axis=0) - one_hot
    slot_index = jnp.sum(before * one_hot, axis=1)
    target = adapter_of * capacity + slot_index
    return (
        jnp.arange(adapter_total * capacity, dtype=jnp.int32)[:, None] == target[None, :]
    ).astype(jnp.bfloat16)


def normalize(field, gain):
    return field / jnp.sqrt(jnp.mean(field * field, axis=-1, keepdims=True) + 1e-06) * gain


def rotate(field, positions):
    half = field.shape[-1] // 2
    freq = jnp.exp(
        -(2.0 * jnp.arange(half, dtype=jnp.float32) / field.shape[-1])
        * jnp.log(jnp.float32(10000.0))
    )
    angle = positions[:, None] * freq[None, :]
    cosine = jnp.cos(angle)[:, None, :]
    sine = jnp.sin(angle)[:, None, :]
    first = field[..., :half]
    second = field[..., half:]
    return jnp.concatenate(
        [first * cosine - second * sine, second * cosine + first * sine], axis=-1
    )


def body(
    tokens,
    query_weight,
    key_weight,
    value_weight,
    query_norm_gain,
    key_norm_gain,
    adapter_down_weight,
    adapter_up_weight,
    token_adapter_index,
    packed_prompt_length,
):
    rows = tokens.shape[0]
    head_dim = query_norm_gain.shape[0]
    kv_local = key_weight.shape[1] // head_dim
    q_local = query_weight.shape[1] // head_dim
    groups = q_local // kv_local
    seq_count = lax.axis_size("seq")
    owned_rows = adapter_down_weight.shape[0]
    adapter_total = owned_rows * seq_count
    capacity = 2 * rows // adapter_total
    feature_slice = adapter_down_weight.shape[1]
    seq_index = lax.axis_index("seq")
    tp_index = lax.axis_index("tp")
    dispatch = make_dispatch(token_adapter_index[:, 0], adapter_total, capacity)
    x_part = lax.dynamic_slice_in_dim(tokens, tp_index * feature_slice, feature_slice, 1)
    packed = jnp.dot(dispatch, x_part, preferred_element_type=jnp.float32).astype(jnp.bfloat16)
    down_all, up_all = (
        lax.all_gather(adapter_down_weight, "seq", axis=0, tiled=True),
        lax.all_gather(adapter_up_weight, "seq", axis=0, tiled=True),
    )
    packed = packed.reshape(adapter_total, capacity, feature_slice)
    partial_low = jnp.einsum("acd,adr->acr", packed, down_all, preferred_element_type=jnp.float32)
    low_rank = lax.psum(partial_low, "tp").astype(jnp.bfloat16)
    delta_slots = jnp.einsum(
        "acr,are->ace", low_rank, up_all, preferred_element_type=jnp.float32
    ).astype(jnp.bfloat16)
    delta_slots = delta_slots.reshape(adapter_total * capacity, q_local * head_dim)
    delta_rows = jnp.einsum("st,se->te", dispatch, delta_slots, preferred_element_type=jnp.float32)
    query = jnp.dot(tokens, query_weight, preferred_element_type=jnp.float32) + delta_rows
    keys = jnp.dot(tokens, key_weight, preferred_element_type=jnp.float32)
    values = jnp.dot(tokens, value_weight, preferred_element_type=jnp.float32).astype(jnp.bfloat16)
    positions = seq_index * rows + jnp.arange(rows, dtype=jnp.int32)
    pos_float = positions.astype(jnp.float32)
    query_rot = rotate(
        normalize(query.reshape(rows, q_local, head_dim), query_norm_gain), pos_float
    ).astype(jnp.bfloat16)
    key_rot = rotate(
        normalize(keys.reshape(rows, kv_local, head_dim), key_norm_gain), pos_float
    ).astype(jnp.bfloat16)
    reach = WINDOW // rows
    earlier = []
    for offset in range(reach, 0, -1):
        earlier.append(passed_along((key_rot, values), "seq", offset))
    all_keys = jnp.concatenate([piece[0] for piece in earlier] + [key_rot], axis=0)
    all_values = jnp.concatenate([piece[1] for piece in earlier] + [values], axis=0)
    all_values = all_values.reshape(WINDOW + rows, kv_local, head_dim)
    key_pos = seq_index * rows - WINDOW + jnp.arange(WINDOW + rows, dtype=jnp.int32)
    starts = jnp.cumsum(packed_prompt_length) - packed_prompt_length
    prompt_start = jnp.max(
        jnp.where(starts[None, :] <= positions[:, None], starts[None, :], 0), axis=1
    )
    lower = jnp.maximum(positions - WINDOW + 1, prompt_start)
    allowed = (key_pos[None, :] >= lower[:, None]) & (key_pos[None, :] <= positions[:, None])
    query_four = query_rot.reshape(rows, kv_local, groups, head_dim)
    scores = (
        jnp.einsum("tkgd,skd->kgts", query_four, all_keys, preferred_element_type=jnp.float32)
        * query_scale
    )
    scores = jnp.where(allowed[None, None], scores, jnp.float32(-1e30))
    peak = jnp.max(scores, axis=-1, keepdims=True)
    weights = jnp.exp(scores - peak)
    probs = (weights / jnp.sum(weights, axis=-1, keepdims=True)).astype(jnp.bfloat16)
    mixed = jnp.einsum("kgts,skd->tkgd", probs, all_values, preferred_element_type=jnp.float32)
    return mixed.astype(jnp.bfloat16).reshape(rows, q_local * head_dim)


def solution(mesh):
    in_specs = (
        P("seq", None),
        P(None, "tp"),
        P(None, "tp"),
        P(None, "tp"),
        P(),
        P(),
        P("seq", "tp", None),
        P("seq", None, "tp"),
        P("seq", None),
        P(),
    )
    out_specs = P("seq", "tp")
    return jax.shard_map(body, mesh=mesh, in_specs=in_specs, out_specs=out_specs, check_vma=False)
```

profile of v0, /device:TPU:8, one launch (start us, length us, event | category | flops | bytes accessed | tf_op | source)
XLA Modules:
  0.0 193.4 jit_solution(9777939212335164480)
XLA Ops:
  6.5 0.0 copy-start
  6.5 0.0 copy-start.5
  6.5 0.0 all-gather.3.cloned.1.call-start
  6.5 0.7 all-gather.3.cloned.1.call-update
  7.3 0.0 all-gather.5.cloned.1.call-start
  7.3 0.0 copy-start.1
  7.4 0.0 copy-start.8
  7.4 5.1 %multiply_reduce_fusion.1 = (f32[512]{0:T(512)S(1)}, f32[512,128]{0,1:T(8,128)S(1)}) fusion(bf16[512,5376]{1,0:T(8,128)(2,1)} %param.10, bf16[5376,128]{1,0:T(8,128)(2,1)} %param.12), kind=kOutput, calls=%fused_computation.43 | convolution fusion | flops 704773632 | bytes 7145472 | tf_op jit(solution)/shard_map/dot_general | solution.py:88
  12.4 0.0 copy-start.4
  12.4 0.0 copy-start.7
  12.5 0.0 copy-done.5
  12.5 0.1 multiply_bitcast_fusion
  12.6 0.6 fusion.34
  13.1 0.0 copy-start.2
  13.2 0.0 copy-start.3
  13.2 0.6 copy-done.2
  13.8 0.7 pad_maximum_fusion
  14.4 0.0 copy-done.3
  14.4 5.8 %collective-permute-start.2 = (bf16[512,1,128]{0,2,1:T(8,128)(2,1)}, bf16[512,1,128]{0,2,1:T(8,128)(2,1)}, u32[]{:S(2)}, u32[]{:S(2)}) collective-permute-start(bf16[512,1,128]{0,2,1:T(8,128)(2,1)} %pad_maximum_fusion), channel_id=1, source_target_pairs={{0,16},{8,24},{16,32},{24,40},{32,48},{40,56},{48,64},{56,72},{64,... | collective-permute-start | bytes 393224 | tf_op jit(solution)/shard_map/ppermute | solution.py:13
  20.2 4.5 %collective-permute-start.3 = (bf16[512,1,128]{0,2,1:T(8,128)(2,1)}, bf16[512,1,128]{0,2,1:T(8,128)(2,1)}, u32[]{:S(2)}, u32[]{:S(2)}) collective-permute-start(bf16[512,1,128]{0,2,1:T(8,128)(2,1)} %pad_maximum_fusion), channel_id=1, source_target_pairs={{0,8},{8,16},{16,24},{24,32},{32,40},{40,48},{48,56},{56,64},{64,7... | collective-permute-start | bytes 393224 | tf_op jit(solution)/shard_map/ppermute | solution.py:13
  24.7 0.0 copy-done.1
  24.7 0.0 copy-done.8
  24.7 2.2 %convolution_convert_fusion.1 = bf16[512,128]{1,0:T(8,128)(2,1)} fusion(bf16[512,5376]{1,0:T(8,128)(2,1)S(1)} %copy-done.1, bf16[5376,128]{1,0:T(8,128)(2,1)S(1)} %copy-done.8), kind=kOutput, calls=%fused_computation.15 | convolution fusion | flops 704708608 | bytes 7012352 | tf_op jit(solution)/shard_map/dot_general | solution.py:89
  27.0 4.9 %collective-permute-start = (bf16[512,128]{1,0:T(8,128)(2,1)}, bf16[512,128]{1,0:T(8,128)(2,1)}, u32[]{:S(2)}, u32[]{:S(2)}) collective-permute-start(bf16[512,128]{1,0:T(8,128)(2,1)} %convolution_convert_fusion.1), channel_id=1, source_target_pairs={{0,16},{8,24},{16,32},{24,40},{32,48},{40,56},{48,64},{56,72},{64,... | collective-permute-start | bytes 393224 | tf_op jit(solution)/shard_map/ppermute | solution.py:13
  31.8 3.6 %collective-permute-start.1 = (bf16[512,128]{1,0:T(8,128)(2,1)}, bf16[512,128]{1,0:T(8,128)(2,1)}, u32[]{:S(2)}, u32[]{:S(2)}) collective-permute-start(bf16[512,128]{1,0:T(8,128)(2,1)} %convolution_convert_fusion.1), channel_id=1, source_target_pairs={{0,8},{8,16},{16,24},{24,32},{32,40},{40,48},{48,56},{56,64},{64,7... | collective-permute-start | bytes 393224 | tf_op jit(solution)/shard_map/ppermute | solution.py:13
  35.4 0.0 all-gather.5.cloned.1.call-update
  35.4 0.0 copy-done.4
  35.5 1.2 reduce-window.20
  36.6 0.2 slice_reduce_fusion
  36.9 0.1 fusion.39
  37.0 0.0 copy-done.7
  37.0 0.1 copy.33
  37.1 0.1 reduce.4
  37.3 3.5 %fusion.6 = bf16[1024,672]{0,1:T(8,128)(2,1)} fusion(s32[512]{0:T(512)S(1)} %multiply_add_fusion, bf16[512,5376]{1,0:T(8,128)(2,1)} %param.10, s32[]{:T(128)S(6)} %select_n.12), kind=kOutput, calls=%fused_computation.11 | convolution fusion | flops 705855488 | bytes 2164740 | tf_op jit(solution)/shard_map/dot_general | solution.py:74
  40.8 0.1 select_reduce_fusion
  40.9 2.5 %copy.35 = bf16[1024,672]{1,0:T(8,128)(2,1)} copy(bf16[1024,672]{0,1:T(8,128)(2,1)} %fusion.6) | data formatting | bytes 2752512 | tf_op jit(solution)/shard_map/convert_element_type | solution.py:74
  43.5 1.8 multiply_cosine_fusion
  45.3 0.7 compare_and_fusion
  45.9 0.0 copy-done
  46.0 5.0 %fusion.47 = f32[512,256]{0,1:T(8,128)} fusion(bf16[512,5376]{1,0:T(8,128)(2,1)} %param.10, bf16[5376,256]{1,0:T(8,128)(2,1)S(1)} %copy-done), kind=kOutput, calls=%fused_computation.78 | convolution fusion | flops 1409286144 | bytes 8781824 | tf_op jit(solution)/shard_map/dot_general | solution.py:87
  51.0 0.0 copy-start.6
  51.0 41.4 %all-gather.3.cloned.1.call-done = bf16[32,672,64]{1,2,0:T(8,128)(2,1)} async-done(((bf16[1,672,64]{1,2,0:T(8,128)(2,1)}), bf16[32,672,64]{1,2,0:T(8,128)(2,1)}) %all-gather.3.cloned.1.call-update) | async-done | bytes 2752528 | tf_op jit(solution)/shard_map/all_gather | solution.py:76
  92.4 4.1 %fusion.48 = f32[32,32,64]{2,1,0:T(8,128)} fusion(bf16[32,32,672]{2,1,0:T(8,128)(2,1)} %bitcast.74, bf16[32,672,64]{1,2,0:T(8,128)(2,1)} %all-gather.3.cloned.1.call-done), kind=kOutput, calls=%fused_computation.79 | convolution fusion | flops 88080384 | bytes 4390912 | tf_op jit(solution)/shard_map/acd,adr->acr/dot_general | solution.py:80
  96.5 27.3 %all-reduce.1 = bf16[32,32,64]{2,1,0:T(8,128)(2,1)} all-reduce(f32[32,32,64]{2,1,0:T(8,128)} %fusion.48), channel_id=1, replica_groups=mesh['seq'=32,'tp'=8] {'tp'}, use_global_device_ids=true, to_apply=%region_6.7 | all-reduce | flops 65536 | bytes 393216 | tf_op jit(solution)/shard_map/psum | solution.py:81
  123.8 44.2 %all-gather.5.cloned.1.call-done = bf16[32,64,256]{2,1,0:T(8,128)(2,1)} async-done(((bf16[1,64,256]{2,1,0:T(8,128)(2,1)}), bf16[32,64,256]{2,1,0:T(8,128)(2,1)}) %all-gather.5.cloned.1.call-update) | async-done | bytes 1048592 | tf_op jit(solution)/shard_map/all_gather | solution.py:77
  167.9 1.6 convolution_convert_fusion
  169.6 2.5 %multiply_reduce_fusion = (f32[512,2]{0,1:T(2,128)S(1)}, f32[512,256]{0,1:T(8,128)}) fusion(f32[512,256]{0,1:T(8,128)} %fusion.47, bf16[1024,256]{1,0:T(8,128)(2,1)S(1)} %bitcast.75, s32[512]{0:T(512)S(1)} %multiply_add_fusion), kind=kOutput, calls=%fused_computation.22 | convolution fusion | flops 269351936 | bytes 1579008 | tf_op jit(solution)/shard_map/st,se->te/dot_general | solution.py:86
  172.0 2.0 %copy.36 = f32[512,2,128]{2,0,1:T(8,128)} copy(f32[512,2,128]{0,2,1:T(8,128)} %bitcast.76) | data formatting | bytes 1048576 | tf_op jit(solution)/shard_map/reshape | solution.py:93
  174.1 0.0 copy-done.6
  174.1 1.2 divide_multiply_fusion
  175.3 1.3 subtract_convert_fusion
  176.6 0.0 collective-permute-done.2
  176.6 0.0 collective-permute-done.3
  176.6 2.7 %fusion.1 = (f32[2,512]{1,0:T(2,128)S(1)}, f32[1536,512,2]{1,0,2:T(8,128)S(1)}) fusion(pred[512,1536]{0,1:T(8,128)(4,1)S(1)} %compare_and_fusion, bf16[512,2,64]{2,0,1:T(8,128)(2,1)S(1)} %get-tuple-element.6, bf16[512,2,64]{2,0,1:T(8,128)(2,1)S(1)} %get-tuple-element.5, bf16[512,1,64]{0,2,1:T(8,128)(2,1)} %copy-done.3, bf16[512,1,64]{0,2,1:T(8,128)(2,1)} %copy-done.2, ...), kind=kOutput, calls=%fused_computation.4 | convolution fusion | flops 409467904 | bytes 7737344 | tf_op jit(solution)/shard_map/tkgd,skd->kgts/dot_general | solution.py:114
  179.3 1.5 fusion
  180.8 0.0 collective-permute-done
  180.8 0.0 collective-permute-done.1
  180.8 3.9 %fusion.8 = bf16[128,2,512]{2,0,1:T(8,128)(2,1)} fusion(f32[2,512]{1,0:T(2,128)S(1)} %fusion, f32[2,512]{1,0:T(2,128)S(1)} %get-tuple-element.15, f32[1536,512,2]{1,0,2:T(8,128)S(1)} %get-tuple-element.16, pred[512,1536]{0,1:T(8,128)(4,1)S(1)} %compare_and_fusion, bf16[512,128]{1,0:T(8,128)(2,1)} %convolution_convert_fusion.1, ...), kind=kOutput, calls=%fused_computation.14 | convolution fusion | flops 411828224 | bytes 7741440 | tf_op jit(solution)/shard_map/kgts,skd->tkgd/dot_general | solution.py:121
  184.7 1.8 copy.40
  (13 shorter events, 0.1 us)
Async XLA Ops:
  6.5 39.4 %copy-start = (bf16[5376,256]{1,0:T(8,128)(2,1)S(1)}, bf16[5376,256]{1,0:T(8,128)(2,1)}, u32[]{:S(2)}) copy-start(bf16[5376,256]{1,0:T(8,128)(2,1)} %param.11) | copy-start | bytes 8257540
  6.5 5.9 %copy-start.5 = (f32[128]{0:T(128)S(1)}, f32[128]{0:T(128)}, u32[]{:S(2)}) copy-start(f32[128]{0:T(128)} %param.15) | copy-start | bytes 1540
  6.5 85.9 %all-gather.3.cloned.1.call-start = ((), (), s32[]{:S(2)}) async-start(), calls=%async_computation | async-start | bytes 3244032 | tf_op jit(solution)/shard_map/all_gather | solution.py:76
  7.3 160.7 %all-gather.5.cloned.1.call-start = ((), (), s32[]{:S(2)}) async-start(), calls=%async_computation.1 | async-start | bytes 1081344 | tf_op jit(solution)/shard_map/all_gather | solution.py:77
  7.3 17.4 %copy-start.1 = (bf16[512,5376]{1,0:T(8,128)(2,1)S(1)}, bf16[512,5376]{1,0:T(8,128)(2,1)}, u32[]{:S(2)}) copy-start(bf16[512,5376]{1,0:T(8,128)(2,1)} %param.10) | copy-start | bytes 16515076
  7.4 17.4 %copy-start.8 = (bf16[5376,128]{1,0:T(8,128)(2,1)S(1)}, bf16[5376,128]{1,0:T(8,128)(2,1)}, u32[]{:S(2)}) copy-start(bf16[5376,128]{1,0:T(8,128)(2,1)} %param.13) | copy-start | bytes 4128772
  12.4 23.0 %copy-start.4 = (s32[512,1]{0,1:T(1,128)S(1)}, s32[512,1]{0,1:T(1,128)}, u32[]{:S(2)}) copy-start(s32[512,1]{0,1:T(1,128)} %param.18) | copy-start | bytes 6148
  12.4 24.6 %copy-start.7 = (s32[16]{0:T(128)S(1)}, s32[16]{0:T(128)}, u32[]{:S(2)}) copy-start(s32[16]{0:T(128)} %param.19) | copy-start | bytes 196
  13.1 0.6 copy-start.2
  13.2 1.3 copy-start.3
  14.4 162.2 %collective-permute-start.2 = (bf16[512,1,128]{0,2,1:T(8,128)(2,1)}, bf16[512,1,128]{0,2,1:T(8,128)(2,1)}, u32[]{:S(2)}, u32[]{:S(2)}) collective-permute-start(bf16[512,1,128]{0,2,1:T(8,128)(2,1)} %pad_maximum_fusion), channel_id=1, source_target_pairs={{0,16},{8,24},{16,32},{24,40},{32,48},{40,56},{48,64},{56,72},{64,... | collective-permute-start | bytes 393224 | tf_op jit(solution)/shard_map/ppermute | solution.py:13
  20.2 156.4 %collective-permute-start.3 = (bf16[512,1,128]{0,2,1:T(8,128)(2,1)}, bf16[512,1,128]{0,2,1:T(8,128)(2,1)}, u32[]{:S(2)}, u32[]{:S(2)}) collective-permute-start(bf16[512,1,128]{0,2,1:T(8,128)(2,1)} %pad_maximum_fusion), channel_id=1, source_target_pairs={{0,8},{8,16},{16,24},{24,32},{32,40},{40,48},{48,56},{56,64},{64,7... | collective-permute-start | bytes 393224 | tf_op jit(solution)/shard_map/ppermute | solution.py:13
  27.0 153.8 %collective-permute-start = (bf16[512,128]{1,0:T(8,128)(2,1)}, bf16[512,128]{1,0:T(8,128)(2,1)}, u32[]{:S(2)}, u32[]{:S(2)}) collective-permute-start(bf16[512,128]{1,0:T(8,128)(2,1)} %convolution_convert_fusion.1), channel_id=1, source_target_pairs={{0,16},{8,24},{16,32},{24,40},{32,48},{40,56},{48,64},{56,72},{64,... | collective-permute-start | bytes 393224 | tf_op jit(solution)/shard_map/ppermute | solution.py:13
  31.8 149.0 %collective-permute-start.1 = (bf16[512,128]{1,0:T(8,128)(2,1)}, bf16[512,128]{1,0:T(8,128)(2,1)}, u32[]{:S(2)}, u32[]{:S(2)}) collective-permute-start(bf16[512,128]{1,0:T(8,128)(2,1)} %convolution_convert_fusion.1), channel_id=1, source_target_pairs={{0,8},{8,16},{16,24},{24,32},{32,40},{40,48},{48,56},{56,64},{64,7... | collective-permute-start | bytes 393224 | tf_op jit(solution)/shard_map/ppermute | solution.py:13
  51.0 123.1 %copy-start.6 = (f32[128]{0:T(128)S(1)}, f32[128]{0:T(128)}, u32[]{:S(2)}) copy-start(f32[128]{0:T(128)} %param.14) | copy-start | bytes 1540
Sparse Core Ops, SparseCore 0:
  9.9 82.4 all-gather.2
  95.0 72.9 all-gather.4
where the time goes:
time: 194 us; the launch traced here: 193 us
  waiting for transfers between devices  86.3 us (44%)
  matrix products  30.6 us (16%)
  blocking collectives  27.3 us (14%)
  starting transfers between devices  18.8 us (10%)
  between operations  13.6 us (7%)
  other arithmetic  9.43 us (5%)
  local copies, waits for them, and re-layouts  7.32 us (4%)
    all_gather x1, waiting for transfers between devices, body(): lax.all_gather(adapter_up_weight, 'seq', axis=0, tiled=True)  44.2 us
    all_gather x1, waiting for transfers between devices, body(): lax.all_gather(adapter_down_weight, 'seq', axis=0, tiled=True)  41.4 us
    psum x1, blocking collectives, body(): low_rank = lax.psum(partial_low, 'tp').astype(jnp.bfloat16)  27.3 us
    ppermute x4, starting transfers between devices, passed_along(): return lax.ppermute(block, axis, route)  18.7 us
    dot_general x1, matrix products, body(): keys = jnp.dot(tokens, key_weight, preferred_element_type=jnp.float32)  5.07 us
    dot_general x1, matrix products, body(): jnp.dot(tokens, query_weight, preferred_element_type=jnp.float32)  5.02 us
    dot_general x1, matrix products, body(): jnp.einsum('acd,adr->acr', packed, down_all, preferred_element_type=jnp.f...  4.11 us
    dot_general x1, matrix products, body(): jnp.einsum('kgts,skd->tkgd', probs, all_values, preferred_element_type=jn...  3.91 us
  transfers between devices with their start and end apart: 6, of which 2 were waited for; matrix products, arithmetic and copies ran while one was open for 21% of the time, Pallas kernels for 0%

commit v1 on v0

--- a/solution.py
+++ b/solution.py
@@ -74,7 +74,10 @@
     packed = jnp.dot(dispatch, x_part, preferred_element_type=jnp.float32).astype(jnp.bfloat16)
     down_all, up_all = (
         lax.all_gather(adapter_down_weight, "seq", axis=0, tiled=True),
-        lax.all_gather(adapter_up_weight, "seq", axis=0, tiled=True),
+        jnp.concatenate(
+            lax.all_to_all(jnp.stack([adapter_up_weight] * lax.axis_size("seq")), "seq", 0, 0),
+            axis=0,
+        ),
     )
     packed = packed.reshape(adapter_total, capacity, feature_slice)
     partial_low = jnp.einsum("acd,adr->acr", packed, down_all, preferred_element_type=jnp.float32)

time: 194 us -> 154 us (0.79)
  the two profiles are of different devices: /device:TPU:8 before, /device:TPU:6 now
where the time goes in v1:
time: 154 us; the launch traced here: 153 us
  waiting for transfers between devices  34.6 us (22%)
  blocking collectives  31.2 us (20%)
  matrix products  30.6 us (20%)
  starting transfers between devices  25.2 us (16%)
  between operations  13.7 us (9%)
  other arithmetic  9.46 us (6%)
  local copies, waits for them, and re-layouts  8.42 us (5%)
    all_gather x1, waiting for transfers between devices, body(): lax.all_gather(adapter_down_weight, 'seq', axis=0, tiled=True)  33.8 us
    psum x1, blocking collectives, body(): low_rank = lax.psum(partial_low, 'tp').astype(jnp.bfloat16)  31.2 us
    ppermute x4, starting transfers between devices, passed_along(): return lax.ppermute(block, axis, route)  17.4 us
    all_to_all x1, starting transfers between devices, body(): lax.all_to_all(jnp.stack([adapter_up_weight] * lax.axis_size('seq')), 'se...  7.77 us
    dot_general x1, matrix products, body(): keys = jnp.dot(tokens, key_weight, preferred_element_type=jnp.float32)  5.07 us
    dot_general x1, matrix products, body(): jnp.dot(tokens, query_weight, preferred_element_type=jnp.float32)  5.01 us
    dot_general x1, matrix products, body(): jnp.einsum('acd,adr->acr', packed, down_all, preferred_element_type=jnp.f...  4.11 us
    dot_general x1, matrix products, body(): jnp.einsum('kgts,skd->tkgd', probs, all_values, preferred_element_type=jn...  3.91 us
  transfers between devices with their start and end apart: 6, of which 1 were waited for; matrix products, arithmetic and copies ran while one was open for 28% of the time, Pallas kernels for 0%

profile of v1, /device:TPU:6, one launch (start us, length us, event | category | flops | bytes accessed | tf_op | source)
XLA Modules:
  0.0 153.2 jit_solution(9365310058817768473)
XLA Ops:
  6.5 0.0 copy-start
  6.5 0.0 copy-start.6
  6.5 0.0 all-gather.2.cloned.1.call-start
  6.5 0.7 all-gather.2.cloned.1.call-update
  7.3 0.0 copy-start.1
  7.3 0.0 copy-start.9
  7.3 5.1 %multiply_reduce_fusion.1 = (f32[512]{0:T(512)S(1)}, f32[512,128]{0,1:T(8,128)S(1)}) fusion(bf16[512,5376]{1,0:T(8,128)(2,1)} %param.10, bf16[5376,128]{1,0:T(8,128)(2,1)} %param.12), kind=kOutput, calls=%fused_computation.44 | convolution fusion | flops 704773632 | bytes 7145472 | tf_op jit(solution)/shard_map/dot_general | solution.py:91
  12.4 0.0 copy-start.4
  12.4 0.0 copy-done.6
  12.4 0.1 multiply_bitcast_fusion
  12.5 0.0 copy-start.5
  12.5 0.6 fusion.35
  13.1 0.0 copy-start.2
  13.1 0.0 copy-start.3
  13.1 0.0 copy-start.8
  13.1 0.6 copy-done.2
  13.7 0.7 pad_maximum_fusion
  14.4 0.0 copy-done.3
  14.4 5.2 %collective-permute-start.2 = (bf16[512,1,128]{0,2,1:T(8,128)(2,1)}, bf16[512,1,128]{0,2,1:T(8,128)(2,1)}, u32[]{:S(2)}, u32[]{:S(2)}) collective-permute-start(bf16[512,1,128]{0,2,1:T(8,128)(2,1)} %pad_maximum_fusion), channel_id=1, source_target_pairs={{0,16},{8,24},{16,32},{24,40},{32,48},{40,56},{48,64},{56,72},{64,... | collective-permute-start | bytes 393224 | tf_op jit(solution)/shard_map/ppermute | solution.py:13
  19.6 3.8 %collective-permute-start.3 = (bf16[512,1,128]{0,2,1:T(8,128)(2,1)}, bf16[512,1,128]{0,2,1:T(8,128)(2,1)}, u32[]{:S(2)}, u32[]{:S(2)}) collective-permute-start(bf16[512,1,128]{0,2,1:T(8,128)(2,1)} %pad_maximum_fusion), channel_id=1, source_target_pairs={{0,8},{8,16},{16,24},{24,32},{32,40},{40,48},{48,56},{56,64},{64,7... | collective-permute-start | bytes 393224 | tf_op jit(solution)/shard_map/ppermute | solution.py:13
  23.4 0.0 copy-done.1
  23.4 0.0 copy-done.9
  23.4 2.2 %convolution_convert_fusion.1 = bf16[512,128]{1,0:T(8,128)(2,1)} fusion(bf16[512,5376]{1,0:T(8,128)(2,1)S(1)} %copy-done.1, bf16[5376,128]{1,0:T(8,128)(2,1)S(1)} %copy-done.9), kind=kOutput, calls=%fused_computation.15 | convolution fusion | flops 704708608 | bytes 7012352 | tf_op jit(solution)/shard_map/dot_general | solution.py:92
  25.7 5.5 %collective-permute-start = (bf16[512,128]{1,0:T(8,128)(2,1)}, bf16[512,128]{1,0:T(8,128)(2,1)}, u32[]{:S(2)}, u32[]{:S(2)}) collective-permute-start(bf16[512,128]{1,0:T(8,128)(2,1)} %convolution_convert_fusion.1), channel_id=1, source_target_pairs={{0,16},{8,24},{16,32},{24,40},{32,48},{40,56},{48,64},{56,72},{64,... | collective-permute-start | bytes 393224 | tf_op jit(solution)/shard_map/ppermute | solution.py:13
  31.1 2.9 %collective-permute-start.1 = (bf16[512,128]{1,0:T(8,128)(2,1)}, bf16[512,128]{1,0:T(8,128)(2,1)}, u32[]{:S(2)}, u32[]{:S(2)}) collective-permute-start(bf16[512,128]{1,0:T(8,128)(2,1)} %convolution_convert_fusion.1), channel_id=1, source_target_pairs={{0,8},{8,16},{16,24},{24,32},{32,40},{40,48},{48,56},{56,64},{64,7... | collective-permute-start | bytes 393224 | tf_op jit(solution)/shard_map/ppermute | solution.py:13
  34.1 0.0 copy-done.4
  34.1 1.1 stack.2
  35.2 7.8 %all-to-all-start = ((bf16[32,1,64,256]{3,2,1,0:T(8,128)(2,1)}), bf16[32,1,64,256]{3,2,1,0:T(8,128)(2,1)}, u32[]{:S(2)}, u32[]{:S(2)}) async-start(bf16[32,1,64,256]{3,2,1,0:T(8,128)(2,1)} %stack.2), calls=%async_computation | async-start | bytes 2097152 | tf_op jit(solution)/shard_map/all_to_all | solution.py:78
  43.0 0.0 copy-done.5
  43.0 1.2 reduce-window.20
  44.2 0.2 slice_reduce_fusion
  44.4 0.0 copy-done.8
  44.4 0.1 copy.33
  44.5 0.1 reduce.4
  44.7 0.1 select_reduce_fusion
  44.8 0.1 fusion.40
  44.9 3.6 %fusion.6 = bf16[1024,672]{0,1:T(8,128)(2,1)} fusion(s32[512]{0:T(512)S(1)} %multiply_add_fusion, bf16[512,5376]{1,0:T(8,128)(2,1)} %param.10, s32[]{:T(128)S(6)} %select_n.12), kind=kOutput, calls=%fused_computation.11 | convolution fusion | flops 705855488 | bytes 2164740 | tf_op jit(solution)/shard_map/dot_general | solution.py:74
  48.4 2.5 %copy.35 = bf16[1024,672]{1,0:T(8,128)(2,1)} copy(bf16[1024,672]{0,1:T(8,128)(2,1)} %fusion.6) | data formatting | bytes 2752512 | tf_op jit(solution)/shard_map/convert_element_type | solution.py:74
  51.0 1.8 %multiply_cosine_fusion = (f32[512,64]{1,0:T(8,128)}, f32[512,64]{1,0:T(8,128)}) fusion(f32[64]{0:T(128)S(1)} %multiply_exponential_fusion, f32[512]{0:T(512)S(1)} %fusion.42), kind=kLoop, calls=%fused_computation.38 | loop fusion | flops 32768 | bytes 264448 | tf_op jit(solution)/shard_map/cos | solution.py:39
  52.8 0.7 compare_and_fusion
  53.5 0.0 copy-done
  53.5 5.0 %fusion.48 = f32[512,256]{0,1:T(8,128)} fusion(bf16[512,5376]{1,0:T(8,128)(2,1)} %param.10, bf16[5376,256]{1,0:T(8,128)(2,1)S(1)} %copy-done), kind=kOutput, calls=%fused_computation.79 | convolution fusion | flops 1409286144 | bytes 8781824 | tf_op jit(solution)/shard_map/dot_general | solution.py:90
  58.5 0.0 copy-start.7
  58.5 33.8 %all-gather.2.cloned.1.call-done = bf16[32,672,64]{1,2,0:T(8,128)(2,1)} async-done(((bf16[1,672,64]{1,2,0:T(8,128)(2,1)}), bf16[32,672,64]{1,2,0:T(8,128)(2,1)}) %all-gather.2.cloned.1.call-update) | async-done | bytes 2752528 | tf_op jit(solution)/shard_map/all_gather | solution.py:76
  92.4 4.1 %fusion.49 = f32[32,32,64]{2,1,0:T(8,128)} fusion(bf16[32,32,672]{2,1,0:T(8,128)(2,1)} %bitcast.77, bf16[32,672,64]{1,2,0:T(8,128)(2,1)} %all-gather.2.cloned.1.call-done), kind=kOutput, calls=%fused_computation.80 | convolution fusion | flops 88080384 | bytes 4390912 | tf_op jit(solution)/shard_map/acd,adr->acr/dot_general | solution.py:83
  96.5 31.2 %all-reduce.1 = bf16[32,32,64]{2,1,0:T(8,128)(2,1)} all-reduce(f32[32,32,64]{2,1,0:T(8,128)} %fusion.49), channel_id=1, replica_groups=mesh['seq'=32,'tp'=8] {'tp'}, use_global_device_ids=true, to_apply=%region_6.7 | all-reduce | flops 65536 | bytes 393216 | tf_op jit(solution)/shard_map/psum | solution.py:84
  127.7 0.0 all-to-all-done
  127.7 1.6 %convolution_convert_fusion = bf16[32,32,256]{2,1,0:T(8,128)(2,1)S(1)} fusion(bf16[32,1,64,256]{3,2,1,0:T(8,128)(2,1)} %all-to-all-done, bf16[32,32,64]{2,1,0:T(8,128)(2,1)} %all-reduce.1), kind=kOutput, calls=%fused_computation.12 | convolution fusion | flops 33816576 | bytes 1703936 | tf_op jit(solution)/shard_map/acr,are->ace/dot_general | solution.py:85
  129.4 2.5 %multiply_reduce_fusion = (f32[512,2]{0,1:T(2,128)S(1)}, f32[512,256]{0,1:T(8,128)}) fusion(f32[512,256]{0,1:T(8,128)} %fusion.48, bf16[1024,256]{1,0:T(8,128)(2,1)S(1)} %bitcast.78, s32[512]{0:T(512)S(1)} %multiply_add_fusion), kind=kOutput, calls=%fused_computation.23 | convolution fusion | flops 269351936 | bytes 1579008 | tf_op jit(solution)/shard_map/st,se->te/dot_general | solution.py:89
  131.8 2.0 %copy.36 = f32[512,2,128]{2,0,1:T(8,128)} copy(f32[512,2,128]{0,2,1:T(8,128)} %bitcast.79) | data formatting | bytes 1048576 | tf_op jit(solution)/shard_map/reshape | solution.py:96
  133.9 0.0 copy-done.7
  133.9 1.2 divide_multiply_fusion
  135.1 1.3 subtract_convert_fusion
  136.4 0.0 collective-permute-done.2
  136.4 0.0 collective-permute-done.3
  136.4 2.7 %fusion.1 = (f32[2,512]{1,0:T(2,128)S(1)}, f32[1536,512,2]{1,0,2:T(8,128)S(1)}) fusion(pred[512,1536]{0,1:T(8,128)(4,1)S(1)} %compare_and_fusion, bf16[512,2,64]{2,0,1:T(8,128)(2,1)S(1)} %get-tuple-element.6, bf16[512,2,64]{2,0,1:T(8,128)(2,1)S(1)} %get-tuple-element.5, bf16[512,1,64]{0,2,1:T(8,128)(2,1)} %copy-done.3, bf16[512,1,64]{0,2,1:T(8,128)(2,1)} %copy-done.2, ...), kind=kOutput, calls=%fused_computation.4 | convolution fusion | flops 409467904 | bytes 7737344 | tf_op jit(solution)/shard_map/tkgd,skd->kgts/dot_general | solution.py:117
  139.1 1.5 fusion
  140.6 0.0 collective-permute-done
  140.6 0.0 collective-permute-done.1
  140.6 3.9 %fusion.8 = bf16[128,2,512]{2,0,1:T(8,128)(2,1)} fusion(f32[2,512]{1,0:T(2,128)S(1)} %fusion, f32[2,512]{1,0:T(2,128)S(1)} %get-tuple-element.15, f32[1536,512,2]{1,0,2:T(8,128)S(1)} %get-tuple-element.16, pred[512,1536]{0,1:T(8,128)(4,1)S(1)} %compare_and_fusion, bf16[512,128]{1,0:T(8,128)(2,1)} %convolution_convert_fusion.1, ...), kind=kOutput, calls=%fused_computation.14 | convolution fusion | flops 411828224 | bytes 7741440 | tf_op jit(solution)/shard_map/kgts,skd->tkgd/dot_general | solution.py:124
  144.5 1.8 %copy.40 = bf16[512,256]{1,0:T(8,128)(2,1)} copy(bf16[512,256]{0,1:T(8,128)(2,1)} %bitcast.80) | data formatting | bytes 524288 | tf_op jit(solution)/shard_map/reshape | solution.py:125
  (13 shorter events, 0.1 us)
Async XLA Ops:
  6.5 47.0 %copy-start = (bf16[5376,256]{1,0:T(8,128)(2,1)S(1)}, bf16[5376,256]{1,0:T(8,128)(2,1)}, u32[]{:S(2)}) copy-start(bf16[5376,256]{1,0:T(8,128)(2,1)} %param.11) | copy-start | bytes 8257540
  6.5 5.9 %copy-start.6 = (f32[128]{0:T(128)S(1)}, f32[128]{0:T(128)}, u32[]{:S(2)}) copy-start(f32[128]{0:T(128)} %param.15) | copy-start | bytes 1540
  6.5 85.9 %all-gather.2.cloned.1.call-start = ((), (), s32[]{:S(2)}) async-start(), calls=%async_computation.1 | async-start | bytes 3244032 | tf_op jit(solution)/shard_map/all_gather | solution.py:76
  7.3 16.1 %copy-start.1 = (bf16[512,5376]{1,0:T(8,128)(2,1)S(1)}, bf16[512,5376]{1,0:T(8,128)(2,1)}, u32[]{:S(2)}) copy-start(bf16[512,5376]{1,0:T(8,128)(2,1)} %param.10) | copy-start | bytes 16515076
  7.3 16.1 %copy-start.9 = (bf16[5376,128]{1,0:T(8,128)(2,1)S(1)}, bf16[5376,128]{1,0:T(8,128)(2,1)}, u32[]{:S(2)}) copy-start(bf16[5376,128]{1,0:T(8,128)(2,1)} %param.13) | copy-start | bytes 4128772
  12.4 21.7 %copy-start.4 = (bf16[1,64,256]{2,1,0:T(8,128)(2,1)S(1)}, bf16[1,64,256]{2,1,0:T(8,128)(2,1)}, u32[]{:S(2)}) copy-start(bf16[1,64,256]{2,1,0:T(8,128)(2,1)} %param.17) | copy-start | bytes 98308
  12.5 30.4 %copy-start.5 = (s32[512,1]{0,1:T(1,128)S(1)}, s32[512,1]{0,1:T(1,128)}, u32[]{:S(2)}) copy-start(s32[512,1]{0,1:T(1,128)} %param.18) | copy-start | bytes 6148
  13.1 0.6 copy-start.2
  13.1 1.3 copy-start.3
  13.1 31.3 %copy-start.8 = (s32[16]{0:T(128)S(1)}, s32[16]{0:T(128)}, u32[]{:S(2)}) copy-start(s32[16]{0:T(128)} %param.19) | copy-start | bytes 196
  14.4 122.0 %collective-permute-start.2 = (bf16[512,1,128]{0,2,1:T(8,128)(2,1)}, bf16[512,1,128]{0,2,1:T(8,128)(2,1)}, u32[]{:S(2)}, u32[]{:S(2)}) collective-permute-start(bf16[512,1,128]{0,2,1:T(8,128)(2,1)} %pad_maximum_fusion), channel_id=1, source_target_pairs={{0,16},{8,24},{16,32},{24,40},{32,48},{40,56},{48,64},{56,72},{64,... | collective-permute-start | bytes 393224 | tf_op jit(solution)/shard_map/ppermute | solution.py:13
  19.6 116.8 %collective-permute-start.3 = (bf16[512,1,128]{0,2,1:T(8,128)(2,1)}, bf16[512,1,128]{0,2,1:T(8,128)(2,1)}, u32[]{:S(2)}, u32[]{:S(2)}) collective-permute-start(bf16[512,1,128]{0,2,1:T(8,128)(2,1)} %pad_maximum_fusion), channel_id=1, source_target_pairs={{0,8},{8,16},{16,24},{24,32},{32,40},{40,48},{48,56},{56,64},{64,7... | collective-permute-start | bytes 393224 | tf_op jit(solution)/shard_map/ppermute | solution.py:13
  25.7 114.9 %collective-permute-start = (bf16[512,128]{1,0:T(8,128)(2,1)}, bf16[512,128]{1,0:T(8,128)(2,1)}, u32[]{:S(2)}, u32[]{:S(2)}) collective-permute-start(bf16[512,128]{1,0:T(8,128)(2,1)} %convolution_convert_fusion.1), channel_id=1, source_target_pairs={{0,16},{8,24},{16,32},{24,40},{32,48},{40,56},{48,64},{56,72},{64,... | collective-permute-start | bytes 393224 | tf_op jit(solution)/shard_map/ppermute | solution.py:13
  31.1 109.5 %collective-permute-start.1 = (bf16[512,128]{1,0:T(8,128)(2,1)}, bf16[512,128]{1,0:T(8,128)(2,1)}, u32[]{:S(2)}, u32[]{:S(2)}) collective-permute-start(bf16[512,128]{1,0:T(8,128)(2,1)} %convolution_convert_fusion.1), channel_id=1, source_target_pairs={{0,8},{8,16},{16,24},{24,32},{32,40},{40,48},{48,56},{56,64},{64,7... | collective-permute-start | bytes 393224 | tf_op jit(solution)/shard_map/ppermute | solution.py:13
  35.2 92.6 %all-to-all-start = ((bf16[32,1,64,256]{3,2,1,0:T(8,128)(2,1)}), bf16[32,1,64,256]{3,2,1,0:T(8,128)(2,1)}, u32[]{:S(2)}, u32[]{:S(2)}) async-start(bf16[32,1,64,256]{3,2,1,0:T(8,128)(2,1)} %stack.2), calls=%async_computation | async-start | bytes 2097152 | tf_op jit(solution)/shard_map/all_to_all | solution.py:78
  58.5 75.3 %copy-start.7 = (f32[128]{0:T(128)S(1)}, f32[128]{0:T(128)}, u32[]{:S(2)}) copy-start(f32[128]{0:T(128)} %param.14) | copy-start | bytes 1540
Sparse Core Ops, SparseCore 0:
  9.9 82.4 all-gather.1
